TPU v7x, 32 devices: a whole 2x2x4 slice. The times are simulated.
32 devices in a mesh: src: 4 (over y, core), tgt: 8 (over z, x).
Axes of the slice: x: 2, y: 2, z: 4, core: 2. Of those that a mesh axis runs over, the one named last changes fastest.
Arguments:
- kernel: bfloat16 [32768, 8192], P('tgt', 'src'), may hold values from -6 to 6
- probes: bfloat16 [3, 64, 8192], P(None, None, 'src'), may hold values from -6 to 6
Outputs:
- middle_basis: float32 [4, 64, 32768], P('src', None, 'tgt')
- coarse_basis: float32 [4, 64, 8, 4096], P(None, None, 'tgt', 'src')
All inputs are finite; a program needn't handle non-finite values.
Results may differ from a plain program's by a relative error of at most 0.0003.
Values sent between devices are 32-bit elements; how exact they have to be, the bound alone decides.
A program may use at most 64 MiB of HBM per device.

v0:
```python
import math

import jax
import jax.numpy as jnp
from jax import lax
from jax.sharding import PartitionSpec as P

highest = lax.Precision.HIGHEST


def from_partner(value, axis, stride):
    mask = 2**stride
    pairs = [(source, source ^ mask) for source in range(lax.axis_size(axis))]
    return lax.ppermute(value, axis, pairs)


def to_targets(local_coarse):
    return lax.all_to_all(local_coarse[None], "src", split_axis=2, concat_axis=0, tiled=True)


def shards(kernel, probes):
    count_tgt = lax.axis_size("tgt")
    scale = math.sqrt(kernel.shape[0] * count_tgt)
    levels, rank, cols = probes.shape
    sketch = lax.dot_general(
        probes.reshape(levels * rank, cols), kernel, (((1,), (1,)), ((), ())),
        preferred_element_type=jnp.float32,
    )
    first, second, third = sketch[:rank], sketch[rank:2 * rank], sketch[2 * rank:]
    shared = sketch[rank:]
    shared = shared + from_partner(shared, "src", 0)
    pair_sum = shared[:rank]
    group_sum = shared[rank:]
    group_sum = group_sum + from_partner(group_sum, "src", 1)
    stack = jnp.concatenate((first, pair_sum, group_sum), axis=0)
    gram = lax.psum(jnp.einsum("rm,sm->rs", stack, stack, precision=highest), "tgt")
    factor = jnp.linalg.cholesky(gram)
    inverse = lax.linalg.triangular_solve(factor, jnp.eye(levels * rank, dtype=jnp.float32), left_side=True, lower=True)
    weights = inverse[rank:] * scale
    bases = jnp.einsum("rs,sm->rm", weights, stack, precision=highest)
    coarse = to_targets(bases[rank:])
    return (bases[:rank][None], coarse[:, :, None, :])


def solution(mesh):
    placed = (P("tgt", "src"), P(None, None, "src"))
    return jax.shard_map(
        shards,
        mesh=mesh,
        in_specs=placed,
        out_specs=(P("src", None, "tgt"), P(None, None, "tgt", "src")),
        check_vma=False,
    )
```

profile of v0, /device:TPU:1, one launch (start us, length us, event | category | flops | bytes accessed | tf_op | source)
XLA Modules:
  0.0 249.8 jit_solution(11995675185659989103)
XLA Ops:
  7.2 1.1 copy-done
  8.3 13.1 %fusion.19 = f32[192,4096]{1,0:T(8,128)} fusion(bf16[192,2048]{1,0:T(8,128)(2,1)S(1)} %bitcast.38, bf16[4096,2048]{1,0:T(8,128)(2,1)} %param.2), kind=kOutput, calls=%fused_computation.48 | convolution fusion | flops 3221225472 | bytes 20709376 | tf_op jit(solution)/shard_map/dot_general | solution.py:25
  21.4 1.9 slice.91
  23.4 4.1 %collective-permute-done = f32[128,4096]{1,0:T(8,128)S(1)} collective-permute-done((f32[128,4096]{1,0:T(8,128)S(1)}, f32[128,4096]{1,0:T(8,128)S(1)}, u32[]{:S(2)}, u32[]{:S(2)}) %collective-permute-start) | collective-permute-done | bytes 2097184 | tf_op jit(solution)/shard_map/ppermute | solution.py:14
  27.9 2.4 collective-permute-start.1
  30.4 23.0 %collective-permute-done.1 = f32[64,4096]{1,0:T(8,128)S(1)} collective-permute-done((f32[64,4096]{1,0:T(8,128)S(1)}, f32[64,4096]{1,0:T(8,128)S(1)}, u32[]{:S(2)}, u32[]{:S(2)}) %collective-permute-start.1) | collective-permute-done | bytes 1048608 | tf_op jit(solution)/shard_map/ppermute | solution.py:14
  53.6 3.4 %fusion.1 = f32[192,192]{0,1:T(8,128)} fusion(f32[64,4096]{1,0:T(8,128)S(1)} %get-tuple-element.25, f32[64,4096]{1,0:T(8,128)S(1)} %get-tuple-element.24, f32[64,4096]{1,0:T(8,128)S(1)} %slice.90), kind=kOutput, calls=%fused_computation.2 | convolution fusion | flops 1813512192 | bytes 3293184 | tf_op jit(solution)/shard_map/rm,sm->rs/dot_general | solution.py:36
  57.1 70.6 %all-reduce.5.cloned.1.call-done = f32[192,192]{0,1:T(8,128)} async-done(((f32[192,192]{0,1:T(8,128)}), f32[192,192]{0,1:T(8,128)}) %all-reduce.5.cloned.1.call-update) | async-done | bytes 147472 | tf_op jit(solution)/shard_map/psum | solution.py:36
  127.7 1.0 copy.8
  128.7 1.0 fusion.2
  129.7 11.7 %cholesky.51 = f32[128,128]{1,0:T(8,128)S(1)} custom-call(f32[128,128]{1,0:T(8,128)S(1)} %cholesky.124), custom_call_target="Cholesky" | custom-call | tf_op jit(solution)/shard_map/jit(cholesky)/cholesky | solution.py:37
  141.4 9.9 %custom-call.14 = f32[1,128,128]{1,2,0:T(8,128)S(1)} custom-call(f32[1,128,128]{2,1,0:T(8,128)S(1)} %get-tuple-element.27), custom_call_target="InvertDiagBlocksLowerTriangular" | custom-call | tf_op jit(solution)/shard_map/jit(cholesky)/cholesky | solution.py:37
  151.8 5.8 %cholesky.110 = f32[64,64]{1,0:T(8,128)S(1)} custom-call(f32[64,64]{1,0:T(8,128)S(1)} %convolution_subtract_fusion.1), custom_call_target="Cholesky" | custom-call | tf_op jit(solution)/shard_map/jit(cholesky)/cholesky | solution.py:37
  157.7 0.7 compare_reduce_fusion
  160.5 19.7 %custom-call.15 = f32[2,128,128]{1,2,0:T(8,128)S(1)} custom-call(f32[2,128,128]{2,1,0:T(8,128)S(1)} %pad_maximum_fusion.3), custom_call_target="InvertDiagBlocksLowerTriangular" | custom-call | tf_op jit(solution)/shard_map/triangular_solve | solution.py:38
  181.1 3.4 %fusion = f32[128,4096]{1,0:T(8,128)S(1)} fusion(f32[64,4096]{1,0:T(8,128)S(1)} %get-tuple-element.25, f32[64,4096]{1,0:T(8,128)S(1)} %get-tuple-element.24, f32[64,4096]{1,0:T(8,128)} %copy-done.2, f32[64,192]{0,1:T(8,128)S(1)} %fusion.13, f32[128,192]{0,1:T(8,128)S(1)} %fusion.3), kind=kOutput, calls=%fused_computation.1 | convolution fusion | flops 1209581568 | bytes 5390336 | tf_op jit(solution)/shard_map/rs,sm->rm/dot_general | solution.py:40
  184.6 1.5 slice_bitcast_fusion
  186.1 4.8 %copy.9 = f32[1,64,4096]{1,0,2:T(1,128)S(1)} copy(f32[1,64,4096]{2,1,0:T(8,128)} %get-tuple-element.22) | data formatting | bytes 2097152 | tf_op jit(solution)/shard_map/broadcast_in_dim | solution.py:18
  191.4 19.3 %reduce.12 = f32[4096,64]{1,0:T(8,128)} reduce(f32[4096,1,64]{2,1,0:T(1,128)S(1)} %bitcast.40, f32[]{:T(128)} %broadcast.136), dimensions={1}, to_apply=%bitcast.28.reduce_sub_computation | reduce | bytes 2097156
  210.8 3.1 %reshape.58 = f32[4,1,65536]{2,1,0:T(1,128)S(1)} reshape(f32[4096,64]{1,0:T(8,128)} %reduce.12) | data formatting | bytes 2097152
  213.9 18.6 %all_to_all.15 = f32[4,1,65536]{2,1,0:T(1,128)S(1)} all-to-all(f32[4,1,65536]{2,1,0:T(1,128)S(1)} %reshape.58), channel_id=1, replica_groups=mesh['src'=4,'tgt'=8] {'src'}, dimensions={0} | all-to-all | bytes 2097152 | tf_op jit(solution)/shard_map/all_to_all | solution.py:18
  232.5 4.6 %reduce.13 = f32[4,65536]{1,0:T(4,128)} reduce(f32[4,1,65536]{2,1,0:T(1,128)S(1)} %all_to_all.15, f32[]{:T(128)} %broadcast.136), dimensions={1}, to_apply=%all_to_all.11.reduce_sub_computation | reduce | bytes 2097156 | tf_op jit(solution)/shard_map/all_to_all | solution.py:18
  237.1 3.8 %reshape.59 = f32[4096,1,64]{2,1,0:T(1,128)S(1)} reshape(f32[4,65536]{1,0:T(4,128)} %reduce.13) | data formatting | bytes 2097152
  240.9 2.1 copy.10
  (30 shorter events, 3.4 us)
Async XLA Ops:
  7.2 1.1 copy-start
  7.2 120.5 %all-reduce.5.cloned.1.call-start = ((), (), s32[]{:S(2)}) async-start(), calls=%async_computation.1 | async-start | bytes 393216 | tf_op jit(solution)/shard_map/psum | solution.py:36
  21.4 6.1 %copy-start.1 = (f32[192,4096]{1,0:T(8,128)S(1)}, f32[192,4096]{1,0:T(8,128)}, u32[]{:S(2)}) copy-start(f32[192,4096]{1,0:T(8,128)} %fusion.19) | copy-start | bytes 9437188
  23.3 4.2 %collective-permute-start = (f32[128,4096]{1,0:T(8,128)S(1)}, f32[128,4096]{1,0:T(8,128)S(1)}, u32[]{:S(2)}, u32[]{:S(2)}) collective-permute-start(f32[128,4096]{1,0:T(8,128)S(1)} %slice.91), channel_id=1, source_target_pairs={{0,8},{8,0},{16,24},{24,16},{1,9},{9,1},{17,25},{25,17},{2,10},{10... | collective-permute-start | bytes 6291464 | tf_op jit(solution)/shard_map/ppermute | solution.py:14
  27.9 25.6 %collective-permute-start.1 = (f32[64,4096]{1,0:T(8,128)S(1)}, f32[64,4096]{1,0:T(8,128)S(1)}, u32[]{:S(2)}, u32[]{:S(2)}) collective-permute-start(f32[64,4096]{1,0:T(8,128)S(1)} %slice.93), channel_id=1, source_target_pairs={{0,16},{8,24},{16,0},{24,8},{1,17},{9,25},{17,1},{25,9},{2,18},{10... | collective-permute-start | bytes 3145736 | tf_op jit(solution)/shard_map/ppermute | solution.py:14
  30.4 23.3 %copy-start.2 = (f32[64,4096]{1,0:T(8,128)}, f32[64,4096]{1,0:T(8,128)S(1)}, u32[]{:S(2)}) copy-start(f32[64,4096]{1,0:T(8,128)S(1)} %slice.90) | copy-start | bytes 3145732
Sparse Core Ops, SparseCore 0:
  57.2 70.4 all-reduce.4
where the time goes:
time: 251 us; the launch traced here: 250 us
  waiting for transfers between devices  97.8 us (39%)
  other arithmetic  74.1 us (30%)
  matrix products  21.2 us (8%)
  local copies, waits for them, and re-layouts  20 us (8%)
  blocking collectives  18.6 us (7%)
  between operations  15.6 us (6%)
  starting transfers between devices  2.55 us (1%)
    psum x1, waiting for transfers between devices, shards(): lax.psum(jnp.einsum('rm,sm->rs', stack, stack, precision=highest), 'tgt')  70.6 us
    another operation x7, other arithmetic, shards(): factor = jnp.linalg.cholesky(gram)  28.9 us
    ppermute x2, waiting for transfers between devices, from_partner(): return lax.ppermute(value, axis, pairs)  27.2 us
    another operation x6, other arithmetic, shards(): lax.linalg.triangular_solve(factor, jnp.eye(levels * rank, dtype=jnp.floa...  19.8 us
    unnamed x1, other arithmetic  19.3 us
    all_to_all x1, blocking collectives, to_targets(): lax.all_to_all(local_coarse[None], 'src', split_axis=2, concat_axis=0, ti...  18.6 us
    dot_general x1, matrix products, shards(): lax.dot_general(probes.reshape(levels * rank, cols), kernel, (((1,), (1,)...  13.1 us
    unnamed x9, local copies, waits for them, and re-layouts  8.53 us
  transfers between devices with their start and end apart: 3, of which 3 were waited for; matrix products, arithmetic and copies ran while one was open for 0% of the time, Pallas kernels for 0%

commit v1 on v0

v1 whole, which is shorter than its diff:
```python
import functools
import math

import jax
import jax.numpy as jnp
from jax import lax
from jax.experimental import pallas as pl
from jax.experimental.pallas import tpu as pltpu
from jax.sharding import PartitionSpec as P

highest = lax.Precision.HIGHEST
MESH = pl.DeviceIdType.MESH
LAG_SHARE, LAG_GROUP, LAG_GRAM = 1, 3, 4


def nt_dot(a, b):
    return lax.dot_general(a, b, (((1,), (1,)), ((), ())), preferred_element_type=jnp.float32)


def split(value):
    high = value.astype(jnp.bfloat16)
    return high, (value - high.astype(jnp.float32)).astype(jnp.bfloat16)


def gather_kernel(n_src, n_tgt, tiles, tile, slots, rank,
                  kernel_hbm, probes_ref, stack_out, gram_out,
                  held, own, shared, stack, chip, total, cross, parts, pieces, summed, full,
                  k_sem, o_sem, a_send, a_recv, b_send, b_recv, c_send, c_recv,
                  r_send, r_recv, g_send, g_recv):
    s = lax.axis_index("src")
    t = lax.axis_index("tgt")
    core = lax.rem(s, 2)
    mate = s + 1 - 2 * core
    pair = lax.rem(s // 2, 2)
    across = s + 2 - 4 * pair
    half = rank // 2

    def fetch(i):
        slot = lax.rem(i, slots)
        return pltpu.make_async_copy(
            kernel_hbm.at[pl.ds(pl.multiple_of(i * tile, tile), tile)], held.at[slot], k_sem.at[slot])

    for i in range(min(slots, tiles)):
        fetch(i).start()

    barrier = pltpu.get_barrier_semaphore()
    pl.semaphore_signal(barrier, inc=1, device_id={"src": mate}, device_id_type=MESH)
    pl.semaphore_signal(barrier, inc=1, device_id={"src": across}, device_id_type=MESH)
    for d in range(1, n_tgt):
        pl.semaphore_signal(barrier, inc=1, device_id={"tgt": lax.rem(t + d, n_tgt)}, device_id_type=MESH)
    pl.semaphore_wait(barrier, n_tgt + 1)

    mine = pl.multiple_of(half * core, half)
    theirs = pl.multiple_of(half * (1 - core), half)

    def remote(src, dst, send, recv, device):
        return pltpu.make_async_remote_copy(
            src_ref=src, dst_ref=dst, send_sem=send, recv_sem=recv, device_id=device, device_id_type=MESH)

    def share_pair(j):
        return remote(own.at[j, pl.ds(rank, rank)], shared.at[j, pl.ds(0, rank)],
                      a_send.at[0, j], a_recv.at[0, j], {"src": mate})

    def share_group(j):
        return remote(own.at[j, pl.ds(2 * rank + theirs, half)], shared.at[j, pl.ds(rank, half)],
                      a_send.at[1, j], a_recv.at[1, j], {"src": mate})

    def cross_chip(j):
        return remote(chip.at[0, j], chip.at[1, j], b_send.at[j], b_recv.at[j], {"src": across})

    def hand_over(j):
        return remote(chip.at[2, j], stack.at[j, pl.ds(2 * rank + mine, half)],
                      c_send.at[j], c_recv.at[j], {"src": mate})

    total[...] = jnp.zeros_like(total)
    cross[...] = jnp.zeros_like(cross)

    def step(i, carry):
        @pl.when(i < tiles)
        def _():
            fetch(i).wait()
            own[i] = nt_dot(probes_ref[...], held[lax.rem(i, slots)])
            share_group(i).start()
            share_pair(i).start()

            @pl.when(i + slots < tiles)
            def _():
                fetch(i + slots).start()

        @pl.when((i >= LAG_SHARE) & (i < tiles + LAG_SHARE))
        def _():
            j = i - LAG_SHARE
            share_group(j).wait_recv()
            chip[0, j] = own[j, pl.ds(2 * rank + mine, half)] + shared[j, rank:rank + half]
            cross_chip(j).start()
            share_pair(j).wait_recv()
            stack[j, 0:rank] = own[j, 0:rank]
            stack[j, rank:2 * rank] = own[j, rank:2 * rank] + shared[j, 0:rank]

        @pl.when((i >= LAG_GROUP) & (i < tiles + LAG_GROUP))
        def _():
            j = i - LAG_GROUP
            cross_chip(j).wait_recv()
            value = chip[0, j] + chip[1, j]
            chip[2, j] = value
            stack[j, pl.ds(2 * rank + mine, half)] = value
            hand_over(j).start()

        @pl.when(i >= LAG_GRAM)
        def _():
            j = i - LAG_GRAM
            hand_over(j).wait_recv()
            high, low = split(stack[j])
            total[...] += nt_dot(high, high)
            cross[...] += nt_dot(high, low)
            pltpu.make_async_copy(stack.at[j], stack_out.at[j], o_sem.at[j]).start()

        return carry

    lax.fori_loop(0, tiles + LAG_GRAM, step, 0)

    mixed = cross[...]
    gram = total[...] + (mixed + mixed.T)
    rows = gram.shape[0] // n_tgt
    for p in range(n_tgt):
        parts[p] = gram[p * rows:(p + 1) * rows]

    scatter = []
    for d in range(1, n_tgt):
        to = lax.rem(t + d, n_tgt)
        scatter.append(remote(parts.at[to], pieces.at[d - 1], r_send.at[d - 1], r_recv.at[d - 1], {"tgt": to}))
        scatter[-1].start()
    value = parts[t]
    for d in range(1, n_tgt):
        scatter[d - 1].wait_recv()
        value = value + pieces[d - 1]
    summed[...] = value
    full[t] = value
    gather = []
    for d in range(1, n_tgt):
        to = lax.rem(t + d, n_tgt)
        gather.append(remote(summed, full.at[t], g_send.at[d - 1], g_recv.at[d - 1], {"tgt": to}))
        gather[-1].start()
    for d in range(1, n_tgt):
        origin = lax.rem(t + n_tgt - d, n_tgt)
        remote(summed, full.at[origin], g_send.at[d - 1], g_recv.at[d - 1], {"tgt": origin}).wait_recv()
    for p in range(n_tgt):
        gram_out[p * rows:(p + 1) * rows, :] = full[p]
    for d in range(1, n_tgt):
        scatter[d - 1].wait_send()
        gather[d - 1].wait_send()

    def finish(j, carry):
        share_group(j).wait_send()
        share_pair(j).wait_send()
        cross_chip(j).wait_send()
        hand_over(j).wait_send()
        pltpu.make_async_copy(stack.at[j], stack_out.at[j], o_sem.at[j]).wait()
        return carry

    lax.fori_loop(0, tiles, finish, 0)


def gather(kernel, probes, tile):
    n_src, n_tgt = lax.axis_size("src"), lax.axis_size("tgt")
    rows, cols = kernel.shape
    total_rank = probes.shape[0]
    rank = total_rank // 3
    tiles = rows // tile
    slots = min(4, tiles)
    f32 = jnp.float32
    dma = pltpu.SemaphoreType.DMA
    return pl.pallas_call(
        functools.partial(gather_kernel, n_src, n_tgt, tiles, tile, slots, rank),
        out_shape=(jax.ShapeDtypeStruct((tiles, total_rank, tile), f32),
                   jax.ShapeDtypeStruct((total_rank, total_rank), f32)),
        in_specs=[pl.BlockSpec(memory_space=pl.ANY), pl.BlockSpec(memory_space=pltpu.VMEM)],
        out_specs=(pl.BlockSpec(memory_space=pl.ANY), pl.BlockSpec(memory_space=pltpu.VMEM)),
        scratch_shapes=[
            pltpu.VMEM((slots, tile, cols), kernel.dtype),
            pltpu.VMEM((tiles, total_rank, tile), f32),
            pltpu.VMEM((tiles, rank + rank // 2, tile), f32),
            pltpu.VMEM((tiles, total_rank, tile), f32),
            pltpu.VMEM((3, tiles, rank // 2, tile), f32),
            pltpu.VMEM((total_rank, total_rank), f32),
            pltpu.VMEM((total_rank, total_rank), f32),
            pltpu.VMEM((n_tgt, total_rank // n_tgt, total_rank), f32),
            pltpu.VMEM((n_tgt - 1, total_rank // n_tgt, total_rank), f32),
            pltpu.VMEM((total_rank // n_tgt, total_rank), f32),
            pltpu.VMEM((n_tgt, total_rank // n_tgt, total_rank), f32),
            dma((slots,)), dma((tiles,)),
            dma((2, tiles)), dma((2, tiles)), dma((tiles,)), dma((tiles,)), dma((tiles,)), dma((tiles,)),
            dma((n_tgt - 1,)), dma((n_tgt - 1,)), dma((n_tgt - 1,)), dma((n_tgt - 1,)),
        ],
        compiler_params=pltpu.CompilerParams(collective_id=0, has_side_effects=True),
        name="gather",
    )(kernel, probes)


def inverse_factor(a, chunk=4):
    n = a.shape[0]
    lanes = 2 * n
    m = jnp.concatenate([a, jnp.eye(n, dtype=a.dtype)], axis=1)
    blocks = [m[8 * r:8 * r + 8] for r in range(n // 8)]
    row_ids = lax.broadcasted_iota(jnp.int32, (8, lanes), 0)
    for start in range(0, n, chunk):
        top = start // 8
        cols = [{r: jnp.broadcast_to(blocks[r][:, start + q:start + q + 1], (8, lanes)) for r in range(top, n // 8)}
                for q in range(chunk)]
        for q in range(chunk):
            inner = (start + q) % 8
            pivot = jnp.broadcast_to(cols[q][top][inner:inner + 1], (8, lanes))
            inv = 1.0 / pivot
            row = jnp.broadcast_to(blocks[top][inner:inner + 1], (8, lanes))
            later = [jnp.broadcast_to(cols[p][top][inner:inner + 1], (8, lanes)) for p in range(q + 1, chunk)]
            row = row * inv
            later = [value * inv for value in later]
            for r in range(top, n // 8):
                mult = cols[q][r]
                if r == top:
                    mult = jnp.where(row_ids > inner, mult, 0.0)
                for p in range(q + 1, chunk):
                    cols[p][r] = cols[p][r] - mult * later[p - q - 1]
                blocks[r] = blocks[r] - mult * row
    m = jnp.concatenate(blocks, axis=0)
    r_ids = lax.broadcasted_iota(jnp.int32, (n, lanes), 0)
    c_ids = lax.broadcasted_iota(jnp.int32, (n, lanes), 1)
    pivots = jnp.sum(jnp.where(r_ids == c_ids, m, 0.0), axis=1, keepdims=True)
    return m[:, n:] * (1.0 / jnp.sqrt(pivots))


def mm(a, b):
    return lax.dot_general(a, b, (((1,), (0,)), ((), ())), precision=highest, preferred_element_type=jnp.float32)


def mmt(a, b):
    return lax.dot_general(a, b, (((1,), (1,)), ((), ())), precision=highest, preferred_element_type=jnp.float32)


def weights_kernel(rank, scale, gram_ref, weights_ref):
    x0 = inverse_factor(gram_ref[0:rank, 0:rank])
    c1 = mmt(gram_ref[rank:, 0:rank], x0)
    rest = gram_ref[rank:, rank:] - mmt(c1, c1)
    x1 = inverse_factor(rest[0:rank, 0:rank])
    c2 = mmt(rest[rank:, 0:rank], x1)
    x2 = inverse_factor(rest[rank:, rank:] - mmt(c2, c2))
    c1x0 = mm(c1, x0)
    mid_first = -mm(x1, c1x0[0:rank])
    weights_ref[0:rank, 0:rank] = scale * mid_first
    weights_ref[0:rank, rank:2 * rank] = scale * x1
    weights_ref[0:rank, 2 * rank:] = jnp.zeros_like(x1)
    weights_ref[rank:, 0:rank] = scale * mm(x2, -c1x0[rank:] - mm(c2, mid_first))
    weights_ref[rank:, rank:2 * rank] = -scale * mm(x2, mm(c2, x1))
    weights_ref[rank:, 2 * rank:] = scale * x2


def weights_of(gram, scale):
    total_rank = gram.shape[0]
    rank = total_rank // 3
    return pl.pallas_call(
        functools.partial(weights_kernel, rank, scale),
        out_shape=jax.ShapeDtypeStruct((2 * rank, total_rank), jnp.float32),
        name="weights",
    )(gram)


def spread_kernel(n_src, tiles, tile, rank, weights_ref, stack_hbm, middle_ref, coarse_ref,
                  stack, wsplit, outgoing, k_sem, send, recv):
    s = lax.axis_index("src")
    per = tiles // n_src

    def fetch(j):
        return pltpu.make_async_copy(stack_hbm.at[j], stack.at[j], k_sem.at[j])

    order = [(lax.rem(s + d + 2, n_src), q) for d in range(n_src) for q in range(per)]
    index = [(to * per + q) for to, q in order]
    for j in index:
        fetch(j).start()

    barrier = pltpu.get_barrier_semaphore()
    for d in range(1, n_src):
        pl.semaphore_signal(barrier, inc=1, device_id={"src": lax.rem(s + d, n_src)}, device_id_type=MESH)
    pl.semaphore_wait(barrier, n_src - 1)

    high, low = split(weights_ref[...])
    wsplit[0:2 * rank] = high
    wsplit[2 * rank:] = low

    def product(j):
        shigh, slow = split(stack[j])
        both = jnp.dot(wsplit[...], shigh, preferred_element_type=jnp.float32)
        return both[0:2 * rank] + (both[2 * rank:] + jnp.dot(wsplit[0:2 * rank], slow, preferred_element_type=jnp.float32))

    copies = []
    for d in range(n_src):
        away = (d + 2) % n_src
        to = lax.rem(s + away, n_src)
        for q in range(per):
            j = to * per + q
            fetch(j).wait()
            value = product(j)
            middle_ref[:, pl.ds(pl.multiple_of(j * tile, tile), tile)] = value[0:rank]
            if away == 0:
                coarse_ref[s, :, q * tile:(q + 1) * tile] = value[rank:]
            else:
                outgoing[(away - 1) * per + q] = value[rank:]
                k = (away - 1) * per + q
                copies.append(pltpu.make_async_remote_copy(
                    src_ref=outgoing.at[k], dst_ref=coarse_ref.at[s, :, pl.ds(q * tile, tile)],
                    send_sem=send.at[k], recv_sem=recv.at[k], device_id={"src": to}, device_id_type=MESH))
                copies[-1].start()
    for away in range(1, n_src):
        origin = lax.rem(s + n_src - away, n_src)
        for q in range(per):
            k = (away - 1) * per + q
            pltpu.make_async_remote_copy(
                src_ref=outgoing.at[k], dst_ref=coarse_ref.at[origin, :, pl.ds(q * tile, tile)],
                send_sem=send.at[k], recv_sem=recv.at[k], device_id={"src": origin}, device_id_type=MESH).wait_recv()
    for copy in copies:
        copy.wait_send()


def spread(weights, stack):
    n_src = lax.axis_size("src")
    tiles, total_rank, tile = stack.shape
    rank = total_rank // 3
    f32 = jnp.float32
    moved = (n_src - 1) * (tiles // n_src)
    dma = pltpu.SemaphoreType.DMA
    return pl.pallas_call(
        functools.partial(spread_kernel, n_src, tiles, tile, rank),
        out_shape=(jax.ShapeDtypeStruct((rank, tiles * tile), f32),
                   jax.ShapeDtypeStruct((n_src, rank, tiles * tile // n_src), f32)),
        in_specs=[pl.BlockSpec(memory_space=pltpu.VMEM), pl.BlockSpec(memory_space=pl.ANY)],
        out_specs=(pl.BlockSpec(memory_space=pltpu.VMEM), pl.BlockSpec(memory_space=pltpu.VMEM)),
        scratch_shapes=[
            pltpu.VMEM((tiles, total_rank, tile), f32),
            pltpu.VMEM((4 * rank, total_rank), jnp.bfloat16),
            pltpu.VMEM((moved, rank, tile), f32),
            dma((tiles,)), dma((moved,)), dma((moved,)),
        ],
        compiler_params=pltpu.CompilerParams(collective_id=1, has_side_effects=True),
        name="spread",
    )(weights, stack)


def shards(kernel, probes):
    n_src, n_tgt = lax.axis_size("src"), lax.axis_size("tgt")
    rows = kernel.shape[0]
    scale = math.sqrt(rows * n_tgt)
    levels, rank, cols = probes.shape
    tile = min(512, rows // n_src)
    stack, gram = gather(kernel, probes.reshape(levels * rank, cols), tile)
    weights = weights_of(gram, scale)
    middle, coarse = spread(weights, stack)
    return (middle[None], coarse[:, :, None, :])


def solution(mesh):
    placed = (P("tgt", "src"), P(None, None, "src"))
    return jax.shard_map(
        shards,
        mesh=mesh,
        in_specs=placed,
        out_specs=(P("src", None, "tgt"), P(None, None, "tgt", "src")),
        check_vma=False,
    )
```

time: 251 us -> 72.4 us (0.29)
  waiting for transfers between devices: 97.8 us -> 0 us
  other arithmetic: 74.1 us -> 0 us
  Pallas kernels: 0 us -> 65.8 us
  matrix products: 21.2 us -> 0 us
  blocking collectives: 18.6 us -> 0 us
  between operations: 15.6 us -> 0.65 us
  local copies, waits for them, and re-layouts: 20 us -> 5.54 us
  starting transfers between devices: 2.55 us -> 0 us
    psum x1 -> x0, waiting for transfers between devices: 70.6 us -> none  [shards(): lax.psum(jnp.einsum('rm,sm->rs', stack, stack, precision=highest), 'tgt')]
    pallas_call x0 -> x3, Pallas kernels: none -> 65.8 us  [the longest x1 36.3 us: gather(): pl.pallas_call(functools.partial(gather_kernel, n_src, n_tgt, tiles, tile...]
    another operation x13 -> x0, other arithmetic: 48.7 us -> none  [the longest x7 28.9 us: shards(): factor = jnp.linalg.cholesky(gram)]
    ppermute x2 -> x0, waiting for transfers between devices: 27.2 us -> none  [from_partner(): return lax.ppermute(value, axis, pairs)]
    dot_general x3 -> x0, matrix products: 19.9 us -> none  [the longest x1 13.1 us: shards(): lax.dot_general(probes.reshape(levels * rank, cols), kernel, (((1,), (1,)...]
    unnamed x1 -> x0, other arithmetic: 19.3 us -> none
    all_to_all x1 -> x0, blocking collectives: 18.6 us -> none  [to_targets(): lax.all_to_all(local_coarse[None], 'src', split_axis=2, concat_axis=0, ti...]
    broadcast_in_dim x2 -> x0, local copies, waits for them, and re-layouts: 6.31 us -> none  [to_targets(): local_coarse[None]]
  transfers between devices with their start and end apart: 3 -> 0, of which waited for: 3 -> 0; matrix products, arithmetic and copies ran while one was open for 0% -> 0% of each run, Pallas kernels for 0% -> 0%
where the time goes in v1:
time: 72.4 us; the launch traced here: 72 us
  Pallas kernels  65.8 us (91%)
  local copies, waits for them, and re-layouts  5.54 us (8%)
    pallas_call x1, Pallas kernels, gather(): pl.pallas_call(functools.partial(gather_kernel, n_src, n_tgt, tiles, tile...  36.3 us
    pallas_call x1, Pallas kernels, spread(): pl.pallas_call(functools.partial(spread_kernel, n_src, tiles, tile, rank)...  17.8 us
    pallas_call x1, Pallas kernels, weights_of(): pl.pallas_call(functools.partial(weights_kernel, rank, scale), out_shape=...  11.8 us
    unnamed x2, local copies, waits for them, and re-layouts  5.54 us

profile of v1, /device:TPU:1, one launch (start us, length us, event | category | flops | bytes accessed | tf_op | source)
XLA Modules:
  0.0 72.0 jit_solution(7778521045386587731)
XLA Ops:
  0.6 36.3 %gather.1 = (f32[8,192,512]{2,1,0:T(8,128)}, f32[192,192]{1,0:T(8,128)}) custom-call(bf16[4096,2048]{1,0:T(8,128)(2,1)} %kernel_hbm.1, bf16[192,2048]{1,0:T(8,128)(2,1)} %bitcast.5), custom_call_target="tpu_custom_call" | custom-call | tf_op jit(solution)/shard_map/gather/pallas_call | solution.py:173
  36.9 11.8 %weights.1.weights_ref = f32[128,192]{1,0:T(8,128)} custom-call(f32[192,192]{1,0:T(8,128)} %get-tuple-element.6.gram_ref), custom_call_target="tpu_custom_call" | custom-call | tf_op jit(solution)/shard_map/weights/pallas_call | solution.py:260
  48.7 17.8 %spread.1 = (f32[64,4096]{1,0:T(8,128)}, f32[4,64,1024]{2,1,0:T(8,128)}) custom-call(f32[128,192]{1,0:T(8,128)} %weights.1.weights_ref, f32[8,192,512]{2,1,0:T(8,128)} %get-tuple-element.7.stack_hbm), custom_call_target="tpu_custom_call" | custom-call | tf_op jit(solution)/shard_map/spread/pallas_call | solution.py:330
  66.5 3.3 %copy.4 = f32[4,64,1,1024]{3,2,1,0:T(1,128)} copy(f32[4,64,1,1024]{3,1,0,2:T(8,128)} %bitcast.4) | data formatting | bytes 2097152
  69.8 2.3 %copy.6 = f32[1,64,4096]{2,1,0:T(8,128)} copy(f32[1,64,4096]{2,1,0:T(8,128)} %bitcast.3) | data formatting | bytes 2097152

commit v2 on v0

v2 whole, which is shorter than its diff:
```python
import functools
import math

import jax
import jax.numpy as jnp
from jax import lax
from jax.experimental import pallas as pl
from jax.experimental.pallas import tpu as pltpu
from jax.sharding import PartitionSpec as P

highest = lax.Precision.HIGHEST
MESH = pl.DeviceIdType.MESH


def nt_dot(a, b):
    return lax.dot_general(a, b, (((1,), (1,)), ((), ())), preferred_element_type=jnp.float32)


def split(value):
    high = value.astype(jnp.bfloat16)
    return high, (value - high.astype(jnp.float32)).astype(jnp.bfloat16)


def inverse_factor(a, chunk=4):
    n = a.shape[0]
    lanes = 2 * n
    m = jnp.concatenate([a, jnp.eye(n, dtype=a.dtype)], axis=1)
    blocks = [m[8 * r:8 * r + 8] for r in range(n // 8)]
    row_ids = lax.broadcasted_iota(jnp.int32, (8, lanes), 0)
    for start in range(0, n, chunk):
        top = start // 8
        cols = [{r: jnp.broadcast_to(blocks[r][:, start + q:start + q + 1], (8, lanes)) for r in range(top, n // 8)}
                for q in range(chunk)]
        for q in range(chunk):
            inner = (start + q) % 8
            pivot = jnp.broadcast_to(cols[q][top][inner:inner + 1], (8, lanes))
            inv = 1.0 / pivot
            row = jnp.broadcast_to(blocks[top][inner:inner + 1], (8, lanes))
            later = [jnp.broadcast_to(cols[p][top][inner:inner + 1], (8, lanes)) for p in range(q + 1, chunk)]
            row = row * inv
            later = [value * inv for value in later]
            for r in range(top, n // 8):
                mult = cols[q][r]
                if r == top:
                    mult = jnp.where(row_ids > inner, mult, 0.0)
                for p in range(q + 1, chunk):
                    cols[p][r] = cols[p][r] - mult * later[p - q - 1]
                blocks[r] = blocks[r] - mult * row
    m = jnp.concatenate(blocks, axis=0)
    r_ids = lax.broadcasted_iota(jnp.int32, (n, lanes), 0)
    c_ids = lax.broadcasted_iota(jnp.int32, (n, lanes), 1)
    pivots = jnp.sum(jnp.where(r_ids == c_ids, m, 0.0), axis=1, keepdims=True)
    return m[:, n:] * (1.0 / jnp.sqrt(pivots))


def mm(a, b):
    return lax.dot_general(a, b, (((1,), (0,)), ((), ())), precision=highest, preferred_element_type=jnp.float32)


def mmt(a, b):
    return lax.dot_general(a, b, (((1,), (1,)), ((), ())), precision=highest, preferred_element_type=jnp.float32)


def flip(index, mask):
    result = 0
    place = 1
    while place <= mask:
        bit = lax.rem(index // place, 2)
        result = result + place * ((1 - bit) if mask & place else bit)
        place *= 2
    return result + (index // place) * place


def remote(src, dst, send, recv, device):
    return pltpu.make_async_remote_copy(
        src_ref=src, dst_ref=dst, send_sem=send, recv_sem=recv, device_id=device, device_id_type=MESH)


class Reduction:
    def __init__(self, n, parts, pieces, summed, full, sems):
        self.n, self.parts, self.pieces, self.summed, self.full = n, parts, pieces, summed, full
        self.r_send, self.r_recv, self.g_send, self.g_recv = (sems.at[k] for k in range(4))
        self.t = lax.axis_index("tgt")

    def scatter(self, value):
        rows = value.shape[0] // self.n
        for p in range(self.n):
            self.parts[p] = value[p * rows:(p + 1) * rows]
        self.sent = []
        for d in range(1, self.n):
            to = lax.rem(self.t + d, self.n)
            self.sent.append(remote(self.parts.at[to], self.pieces.at[d - 1],
                                    self.r_send.at[d - 1], self.r_recv.at[d - 1], {"tgt": to}))
            self.sent[-1].start()

    def gather(self):
        value = self.parts[self.t]
        for d in range(1, self.n):
            self.sent[d - 1].wait_recv()
            value = value + self.pieces[d - 1]
        self.summed[...] = value
        self.full[self.t] = value
        for d in range(1, self.n):
            to = lax.rem(self.t + d, self.n)
            self.sent.append(remote(self.summed, self.full.at[self.t],
                                    self.g_send.at[d - 1], self.g_recv.at[d - 1], {"tgt": to}))
            self.sent[-1].start()

    def result(self):
        for d in range(1, self.n):
            origin = lax.rem(self.t + self.n - d, self.n)
            remote(self.summed, self.full.at[origin], self.g_send.at[d - 1], self.g_recv.at[d - 1],
                   {"tgt": origin}).wait_recv()
        return jnp.concatenate([self.full[p] for p in range(self.n)], axis=0)

    def drain(self):
        for copy in self.sent:
            copy.wait_send()


def moved_rows(mask, rank):
    return rank * (3 if mask % 4 == 0 else 2 if mask % 2 == 0 else 1)


def gather_kernel(n_src, n_tgt, tiles, tile, slots, rank, scale,
                  kernel_hbm, probes_ref, stack_out, moved_out, middle_out, coarse_out,
                  held, own, shared, stack, chip, total, cross,
                  parts_a, pieces_a, summed_a, full_a, parts_b, pieces_b, summed_b, full_b,
                  k_sem, o_sem, a_send, a_recv, b_send, b_recv, c_send, c_recv,
                  ra_sems, rb_sems, m_send, m_recv, w_send, w_recv):
    s = lax.axis_index("src")
    t = lax.axis_index("tgt")
    core = lax.rem(s, 2)
    mate = flip(s, 1)
    across = flip(s, 2)
    half = rank // 2
    per = tiles // n_src

    def fetch(i):
        slot = lax.rem(i, slots)
        return pltpu.make_async_copy(
            kernel_hbm.at[pl.ds(pl.multiple_of(i * tile, tile), tile)], held.at[slot], k_sem.at[slot])

    for i in range(min(slots, tiles)):
        fetch(i).start()

    barrier = pltpu.get_barrier_semaphore()
    for mask in range(1, n_src):
        pl.semaphore_signal(barrier, inc=1, device_id={"src": flip(s, mask)}, device_id_type=MESH)
    for d in range(1, n_tgt):
        pl.semaphore_signal(barrier, inc=1, device_id={"tgt": lax.rem(t + d, n_tgt)}, device_id_type=MESH)
    pl.semaphore_wait(barrier, n_tgt + n_src - 2)

    mine = pl.multiple_of(half * core, half)
    theirs = pl.multiple_of(half * (1 - core), half)

    def share_pair(j):
        return remote(own.at[j, pl.ds(rank, rank)], shared.at[j, pl.ds(0, rank)],
                      a_send.at[0, j], a_recv.at[0, j], {"src": mate})

    def share_group(j):
        return remote(own.at[j, pl.ds(2 * rank + theirs, half)], shared.at[j, pl.ds(rank, half)],
                      a_send.at[1, j], a_recv.at[1, j], {"src": mate})

    def cross_chip(j):
        return remote(chip.at[0, j], chip.at[1, j], b_send.at[j], b_recv.at[j], {"src": across})

    def hand_over(j):
        return remote(chip.at[2, j], stack.at[j, pl.ds(2 * rank + mine, half)],
                      c_send.at[j], c_recv.at[j], {"src": mate})

    def move(mask, q):
        to = flip(s, mask)
        count = moved_rows(mask, rank)
        return remote(stack.at[to * per + q, pl.ds(0, count)], moved_out.at[mask - 1, q, pl.ds(0, count)],
                      m_send.at[mask - 1, q], m_recv.at[mask - 1, q], {"src": to})

    def save(j):
        return pltpu.make_async_copy(stack.at[j], stack_out.at[j], o_sem.at[j])

    total[...] = jnp.zeros_like(total)
    cross[...] = jnp.zeros_like(cross)

    def step(i, carry):
        @pl.when(i < tiles)
        def _():
            fetch(i).wait()
            own[i] = nt_dot(probes_ref[...], held[lax.rem(i, slots)])
            share_group(i).start()
            share_pair(i).start()

            @pl.when(i + slots < tiles)
            def _():
                fetch(i + slots).start()

        @pl.when(i >= 1)
        def _():
            j = i - 1
            share_group(j).wait_recv()
            chip[0, j] = own[j, pl.ds(2 * rank + mine, half)] + shared[j, rank:rank + half]
            cross_chip(j).start()
            share_pair(j).wait_recv()
            first = own[j, 0:rank]
            second = own[j, rank:2 * rank] + shared[j, 0:rank]
            both = jnp.concatenate([first, second], axis=0)
            stack[j, 0:2 * rank] = both
            high, low = split(both)
            total[...] += nt_dot(high, high)
            cross[...] += nt_dot(high, low)

        return carry

    lax.fori_loop(0, tiles + 1, step, 0)

    lower = Reduction(n_tgt, parts_a, pieces_a, summed_a, full_a, ra_sems)
    mixed = cross[...]
    lower.scatter(total[...] + (mixed + mixed.T))
    late = []
    for mask in (2, 3, 1) + tuple(range(4, n_src)):
        for q in range(per):
            if mask % 4 == 0:
                late.append((mask, q))
            else:
                move(mask, q).start()

    def group(j, carry):
        cross_chip(j).wait_recv()
        value = chip[0, j] + chip[1, j]
        chip[2, j] = value
        stack[j, pl.ds(2 * rank + mine, half)] = value
        hand_over(j).start()
        return carry

    early = (tiles * 3) // 4
    lax.fori_loop(0, early, group, 0)
    lower.gather()
    lax.fori_loop(early, tiles, group, 0)

    def upper_gram(j, carry):
        hand_over(j).wait_recv()
        save(j).start()
        high, low = split(stack[j])
        top = high[2 * rank:]
        return carry + (nt_dot(top, high) + (nt_dot(top, low) + nt_dot(low[2 * rank:], high)))

    upper_value = lax.fori_loop(0, tiles, upper_gram, jnp.zeros((rank, 3 * rank), jnp.float32))
    for mask, q in late:
        move(mask, q).start()
    upper = Reduction(n_tgt, parts_b, pieces_b, summed_b, full_b, rb_sems)
    upper.scatter(upper_value)

    low_gram = lower.result()
    x0 = inverse_factor(low_gram[0:rank, 0:rank])
    c_pair = mmt(low_gram[rank:, 0:rank], x0)
    rest = low_gram[rank:, rank:] - mmt(c_pair, c_pair)
    upper.gather()
    x1 = inverse_factor(rest)
    mid_first = -mm(x1, mm(c_pair, x0))
    middle_out[:, 0:rank] = scale * mid_first
    middle_out[:, rank:] = scale * x1
    up_gram = upper.result()
    c_first = mmt(up_gram[:, 0:rank], x0)
    c_mid = mmt(up_gram[:, rank:2 * rank] - mmt(c_first, c_pair), x1)
    x2 = inverse_factor(up_gram[:, 2 * rank:] - mmt(c_first, c_first) - mmt(c_mid, c_mid))
    coarse_out[0, :, 0:rank] = -scale * mm(x2, mm(c_first, x0) + mm(c_mid, mid_first))
    coarse_out[0, :, rank:2 * rank] = -scale * mm(x2, mm(c_mid, x1))
    coarse_out[0, :, 2 * rank:] = scale * x2

    def tell(mask):
        return remote(coarse_out.at[0], coarse_out.at[mask], w_send.at[mask - 1], w_recv.at[mask - 1],
                      {"src": flip(s, mask)})

    for mask in range(1, n_src):
        tell(mask).start()

    lower.drain()
    upper.drain()

    def finish(j, carry):
        share_group(j).wait_send()
        share_pair(j).wait_send()
        cross_chip(j).wait_send()
        hand_over(j).wait_send()
        save(j).wait()
        return carry

    lax.fori_loop(0, tiles, finish, 0)
    for mask in range(1, n_src):
        for q in range(per):
            move(mask, q).wait()
    for mask in range(1, n_src):
        tell(mask).wait()


def gather(kernel, probes, tile, scale):
    n_src, n_tgt = lax.axis_size("src"), lax.axis_size("tgt")
    rows, cols = kernel.shape
    total_rank = probes.shape[0]
    rank = total_rank // 3
    tiles = rows // tile
    per = tiles // n_src
    slots = min(4, tiles)
    f32 = jnp.float32
    dma = pltpu.SemaphoreType.DMA
    low, up = 2 * rank, rank
    return pl.pallas_call(
        functools.partial(gather_kernel, n_src, n_tgt, tiles, tile, slots, rank, scale),
        out_shape=(jax.ShapeDtypeStruct((tiles, total_rank, tile), f32),
                   jax.ShapeDtypeStruct((n_src - 1, per, total_rank, tile), f32),
                   jax.ShapeDtypeStruct((rank, 2 * rank), f32),
                   jax.ShapeDtypeStruct((n_src, rank, total_rank), f32)),
        in_specs=[pl.BlockSpec(memory_space=pl.ANY), pl.BlockSpec(memory_space=pltpu.VMEM)],
        out_specs=(pl.BlockSpec(memory_space=pl.ANY), pl.BlockSpec(memory_space=pl.ANY),
                   pl.BlockSpec(memory_space=pltpu.VMEM), pl.BlockSpec(memory_space=pltpu.VMEM)),
        scratch_shapes=[
            pltpu.VMEM((slots, tile, cols), kernel.dtype),
            pltpu.VMEM((tiles, total_rank, tile), f32),
            pltpu.VMEM((tiles, rank + rank // 2, tile), f32),
            pltpu.VMEM((tiles, total_rank, tile), f32),
            pltpu.VMEM((3, tiles, rank // 2, tile), f32),
            pltpu.VMEM((low, low), f32),
            pltpu.VMEM((low, low), f32),
            pltpu.VMEM((n_tgt, low // n_tgt, low), f32),
            pltpu.VMEM((n_tgt - 1, low // n_tgt, low), f32),
            pltpu.VMEM((low // n_tgt, low), f32),
            pltpu.VMEM((n_tgt, low // n_tgt, low), f32),
            pltpu.VMEM((n_tgt, up // n_tgt, total_rank), f32),
            pltpu.VMEM((n_tgt - 1, up // n_tgt, total_rank), f32),
            pltpu.VMEM((up // n_tgt, total_rank), f32),
            pltpu.VMEM((n_tgt, up // n_tgt, total_rank), f32),
            dma((slots,)), dma((tiles,)),
            dma((2, tiles)), dma((2, tiles)), dma((tiles,)), dma((tiles,)), dma((tiles,)), dma((tiles,)),
            dma((4, n_tgt - 1)), dma((4, n_tgt - 1)),
            dma((n_src - 1, per)), dma((n_src - 1, per)), dma((n_src - 1,)), dma((n_src - 1,)),
        ],
        compiler_params=pltpu.CompilerParams(collective_id=0, has_side_effects=True),
        name="gather",
    )(kernel, probes)


def finish_kernel(n_src, tiles, tile, rank, stack_hbm, moved_hbm, middle_w, coarse_w, middle_ref, coarse_ref,
                  stack, moved, mine, s_sem, m_sem, o_sem):
    s = lax.axis_index("src")
    per = tiles // n_src

    def fetch(j):
        return pltpu.make_async_copy(stack_hbm.at[j, pl.ds(0, 2 * rank)], stack.at[j], s_sem.at[j])

    def fetch_mine(q):
        return pltpu.make_async_copy(stack_hbm.at[s * per + q], mine.at[q], o_sem.at[q])

    def fetch_moved(mask, q):
        count = moved_rows(mask, rank)
        return pltpu.make_async_copy(moved_hbm.at[mask - 1, q, pl.ds(0, count)],
                                     moved.at[mask - 1, q, pl.ds(0, count)], m_sem.at[mask - 1, q])

    for q in range(per):
        fetch_mine(q).start()
    for mask in range(1, n_src):
        for q in range(per):
            fetch_moved(mask, q).start()
    for j in range(tiles):
        fetch(j).start()

    def product(weights, operand):
        w_high, w_low = split(weights)
        high, low = split(operand)
        count = weights.shape[0]
        both = jnp.dot(jnp.concatenate([w_high, w_low], axis=0), high, preferred_element_type=jnp.float32)
        return both[:count] + (both[count:] + jnp.dot(w_high, low, preferred_element_type=jnp.float32))

    for q in range(per):
        fetch_mine(q).wait()
    for mask in range(n_src):
        for q in range(per):
            if mask:
                fetch_moved(mask, q).wait()

            def rows(source, index):
                ref = moved.at[source - 1, q] if source else mine.at[q]
                return ref[index * rank:(index + 1) * rank]

            operand = jnp.concatenate(
                [rows(mask, 0), rows(mask - mask % 2, 1), rows(mask - mask % 4, 2)], axis=0)
            coarse_ref[flip(s, mask), :, 0, q * tile:(q + 1) * tile] = product(coarse_w[mask], operand)
    for j in range(tiles):
        fetch(j).wait()
        middle_ref[0, :, j * tile:(j + 1) * tile] = product(middle_w[...], stack[j])


def finish(stack, moved, middle_w, coarse_w):
    n_src = lax.axis_size("src")
    tiles, total_rank, tile = stack.shape
    rank = total_rank // 3
    per = tiles // n_src
    f32 = jnp.float32
    dma = pltpu.SemaphoreType.DMA
    vmem = pl.BlockSpec(memory_space=pltpu.VMEM)
    hbm = pl.BlockSpec(memory_space=pl.ANY)
    return pl.pallas_call(
        functools.partial(finish_kernel, n_src, tiles, tile, rank),
        out_shape=(jax.ShapeDtypeStruct((1, rank, tiles * tile), f32),
                   jax.ShapeDtypeStruct((n_src, rank, 1, per * tile), f32)),
        in_specs=[hbm, hbm, vmem, vmem],
        out_specs=(vmem, vmem),
        scratch_shapes=[
            pltpu.VMEM((tiles, 2 * rank, tile), f32),
            pltpu.VMEM((n_src - 1, per, total_rank, tile), f32),
            pltpu.VMEM((per, total_rank, tile), f32),
            dma((tiles,)), dma((n_src - 1, per)), dma((per,)),
        ],
        name="finish",
    )(stack, moved, middle_w, coarse_w)


def shards(kernel, probes):
    n_src, n_tgt = lax.axis_size("src"), lax.axis_size("tgt")
    rows = kernel.shape[0]
    scale = math.sqrt(rows * n_tgt)
    levels, rank, cols = probes.shape
    tile = min(512, rows // n_src)
    return finish(*gather(kernel, probes.reshape(levels * rank, cols), tile, scale))


def solution(mesh):
    placed = (P("tgt", "src"), P(None, None, "src"))
    return jax.shard_map(
        shards,
        mesh=mesh,
        in_specs=placed,
        out_specs=(P("src", None, "tgt"), P(None, None, "tgt", "src")),
        check_vma=False,
    )
```

time: 251 us -> 54.1 us (0.22)
  waiting for transfers between devices: 97.8 us -> 0 us
  other arithmetic: 74.1 us -> 0 us
  Pallas kernels: 0 us -> 53.2 us
  matrix products: 21.2 us -> 0 us
  local copies, waits for them, and re-layouts: 20 us -> 0 us
  blocking collectives: 18.6 us -> 0 us
  between operations: 15.6 us -> 0.64 us
  starting transfers between devices: 2.55 us -> 0 us
    psum x1 -> x0, waiting for transfers between devices: 70.6 us -> none  [shards(): lax.psum(jnp.einsum('rm,sm->rs', stack, stack, precision=highest), 'tgt')]
    pallas_call x0 -> x2, Pallas kernels: none -> 53.2 us  [the longest x1 45.8 us: gather(): pl.pallas_call(functools.partial(gather_kernel, n_src, n_tgt, tiles, tile...]
    another operation x13 -> x0, other arithmetic: 48.7 us -> none  [the longest x7 28.9 us: shards(): factor = jnp.linalg.cholesky(gram)]
    ppermute x2 -> x0, waiting for transfers between devices: 27.2 us -> none  [from_partner(): return lax.ppermute(value, axis, pairs)]
    dot_general x3 -> x0, matrix products: 19.9 us -> none  [the longest x1 13.1 us: shards(): lax.dot_general(probes.reshape(levels * rank, cols), kernel, (((1,), (1,)...]
    unnamed x1 -> x0, other arithmetic: 19.3 us -> none
    all_to_all x1 -> x0, blocking collectives: 18.6 us -> none  [to_targets(): lax.all_to_all(local_coarse[None], 'src', split_axis=2, concat_axis=0, ti...]
    unnamed x9 -> x0, local copies, waits for them, and re-layouts: 8.53 us -> none
  transfers between devices with their start and end apart: 3 -> 0, of which waited for: 3 -> 0; matrix products, arithmetic and copies ran while one was open for 0% -> 0% of each run, Pallas kernels for 0% -> 0%
where the time goes in v2:
time: 54.1 us; the launch traced here: 53.9 us
  Pallas kernels  53.2 us (98%)
  between operations  0.64 us (1%)
    pallas_call x1, Pallas kernels, gather(): pl.pallas_call(functools.partial(gather_kernel, n_src, n_tgt, tiles, tile...  45.8 us
    pallas_call x1, Pallas kernels, finish(): pl.pallas_call(functools.partial(finish_kernel, n_src, tiles, tile, rank)...  7.45 us

profile of v2, /device:TPU:1, one launch (start us, length us, event | category | flops | bytes accessed | tf_op | source)
XLA Modules:
  0.0 53.9 jit_solution(7925341897248611068)
XLA Ops:
  0.6 45.8 %gather.1 = (f32[8,192,512]{2,1,0:T(8,128)}, f32[3,2,192,512]{3,2,1,0:T(8,128)}, f32[64,128]{1,0:T(8,128)}, f32[4,64,192]{2,1,0:T(8,128)}) custom-call(bf16[4096,2048]{1,0:T(8,128)(2,1)} %kernel_hbm.1, bf16[192,2048]{1,0:T(8,128)(2,1)} %bitcast.1), custom_call_target="tpu_custom_call" | custom-call | tf_op jit(solution)/shard_map/gather/pallas_call | solution.py:306
  46.4 7.4 %finish.1 = (f32[1,64,4096]{2,1,0:T(8,128)}, f32[4,64,1,1024]{3,2,1,0:T(1,128)}) custom-call(f32[8,192,512]{2,1,0:T(8,128)} %get-tuple-element.6.stack_hbm, f32[3,2,192,512]{3,2,1,0:T(8,128)} %get-tuple-element.7.moved_hbm, f32[64,128]{1,0:T(8,128)} %get-tuple-element.8.middle_w, f32[4,64,192]{2,1,0:T(8,128)} %get-tuple-element.9.coarse_w), custom_call_target="tpu_custom_call" | custom-call | tf_op jit(solution)/shard_map/finish/pallas_call | solution.py:400

commit v3 on v2

--- a/solution.py
+++ b/solution.py
@@ -231,7 +231,7 @@
         hand_over(j).start()
         return carry
 
-    early = (tiles * 3) // 4
+    early = tiles // 2
     lax.fori_loop(0, early, group, 0)
     lower.gather()
     lax.fori_loop(early, tiles, group, 0)
@@ -339,7 +339,7 @@
 
 
 def finish_kernel(n_src, tiles, tile, rank, stack_hbm, moved_hbm, middle_w, coarse_w, middle_ref, coarse_ref,
-                  stack, moved, mine, s_sem, m_sem, o_sem):
+                  stack, moved, mine, middle, coarse, s_sem, m_sem, o_sem, mo_sem, co_sem):
     s = lax.axis_index("src")
     per = tiles // n_src
 
@@ -362,6 +362,12 @@
     for j in range(tiles):
         fetch(j).start()
 
+    def put_coarse(mask):
+        return pltpu.make_async_copy(coarse.at[mask], coarse_ref.at[flip(s, mask)], co_sem.at[mask])
+
+    def put_middle(j):
+        return pltpu.make_async_copy(middle.at[j], middle_ref.at[0, :, pl.ds(j * tile, tile)], mo_sem.at[j])
+
     def product(weights, operand):
         w_high, w_low = split(weights)
         high, low = split(operand)
@@ -382,10 +388,16 @@
 
             operand = jnp.concatenate(
                 [rows(mask, 0), rows(mask - mask % 2, 1), rows(mask - mask % 4, 2)], axis=0)
-            coarse_ref[flip(s, mask), :, 0, q * tile:(q + 1) * tile] = product(coarse_w[mask], operand)
+            coarse[mask, :, 0, q * tile:(q + 1) * tile] = product(coarse_w[mask], operand)
+        put_coarse(mask).start()
     for j in range(tiles):
         fetch(j).wait()
-        middle_ref[0, :, j * tile:(j + 1) * tile] = product(middle_w[...], stack[j])
+        middle[j] = product(middle_w[...], stack[j])
+        put_middle(j).start()
+    for mask in range(n_src):
+        put_coarse(mask).wait()
+    for j in range(tiles):
+        put_middle(j).wait()
 
 
 def finish(stack, moved, middle_w, coarse_w):
@@ -402,12 +414,14 @@
         out_shape=(jax.ShapeDtypeStruct((1, rank, tiles * tile), f32),
                    jax.ShapeDtypeStruct((n_src, rank, 1, per * tile), f32)),
         in_specs=[hbm, hbm, vmem, vmem],
-        out_specs=(vmem, vmem),
+        out_specs=(hbm, hbm),
         scratch_shapes=[
             pltpu.VMEM((tiles, 2 * rank, tile), f32),
             pltpu.VMEM((n_src - 1, per, total_rank, tile), f32),
             pltpu.VMEM((per, total_rank, tile), f32),
-            dma((tiles,)), dma((n_src - 1, per)), dma((per,)),
+            pltpu.VMEM((tiles, rank, tile), f32),
+            pltpu.VMEM((n_src, rank, 1, per * tile), f32),
+            dma((tiles,)), dma((n_src - 1, per)), dma((per,)), dma((tiles,)), dma((n_src,)),
         ],
         name="finish",
     )(stack, moved, middle_w, coarse_w)

time: 54.1 us -> 53.7 us (level)
  no operation moved by 1% of the time
where the time goes in v3:
time: 53.7 us; the launch traced here: 53.5 us
  Pallas kernels  52.9 us (99%)
  between operations  0.64 us (1%)
    pallas_call x1, Pallas kernels, gather(): pl.pallas_call(functools.partial(gather_kernel, n_src, n_tgt, tiles, tile...  45.8 us
    pallas_call x1, Pallas kernels, finish(): pl.pallas_call(functools.partial(finish_kernel, n_src, tiles, tile, rank)...  7.1 us

profile of v3, /device:TPU:1, one launch (start us, length us, event | category | flops | bytes accessed | tf_op | source)
XLA Modules:
  0.0 53.5 jit_solution(5215113471418517660)
XLA Ops:
  0.6 45.8 %gather.1 = (f32[8,192,512]{2,1,0:T(8,128)}, f32[3,2,192,512]{3,2,1,0:T(8,128)}, f32[64,128]{1,0:T(8,128)}, f32[4,64,192]{2,1,0:T(8,128)}) custom-call(bf16[4096,2048]{1,0:T(8,128)(2,1)} %kernel_hbm.1, bf16[192,2048]{1,0:T(8,128)(2,1)} %bitcast.1), custom_call_target="tpu_custom_call" | custom-call | tf_op jit(solution)/shard_map/gather/pallas_call | solution.py:306
  46.4 7.1 %finish.1 = (f32[1,64,4096]{2,1,0:T(8,128)}, f32[4,64,1,1024]{3,2,1,0:T(1,128)}) custom-call(f32[8,192,512]{2,1,0:T(8,128)} %get-tuple-element.6.stack_hbm, f32[3,2,192,512]{3,2,1,0:T(8,128)} %get-tuple-element.7.moved_hbm, f32[64,128]{1,0:T(8,128)} %get-tuple-element.8.middle_w, f32[4,64,192]{2,1,0:T(8,128)} %get-tuple-element.9.coarse_w), custom_call_target="tpu_custom_call" | custom-call | tf_op jit(solution)/shard_map/finish/pallas_call | solution.py:412

commit v4 on v3

--- a/solution.py
+++ b/solution.py
@@ -124,7 +124,7 @@
 
 def gather_kernel(n_src, n_tgt, tiles, tile, slots, rank, scale,
                   kernel_hbm, probes_ref, stack_out, moved_out, middle_out, coarse_out,
-                  held, own, shared, stack, chip, total, cross,
+                  held, own, shared, stack, chip, total,
                   parts_a, pieces_a, summed_a, full_a, parts_b, pieces_b, summed_b, full_b,
                   k_sem, o_sem, a_send, a_recv, b_send, b_recv, c_send, c_recv,
                   ra_sems, rb_sems, m_send, m_recv, w_send, w_recv):
@@ -179,7 +179,6 @@
         return pltpu.make_async_copy(stack.at[j], stack_out.at[j], o_sem.at[j])
 
     total[...] = jnp.zeros_like(total)
-    cross[...] = jnp.zeros_like(cross)
 
     def step(i, carry):
         @pl.when(i < tiles)
@@ -205,16 +204,15 @@
             both = jnp.concatenate([first, second], axis=0)
             stack[j, 0:2 * rank] = both
             high, low = split(both)
-            total[...] += nt_dot(high, high)
-            cross[...] += nt_dot(high, low)
+            total[...] += nt_dot(high, jnp.concatenate([high, low], axis=0))
 
         return carry
 
     lax.fori_loop(0, tiles + 1, step, 0)
 
     lower = Reduction(n_tgt, parts_a, pieces_a, summed_a, full_a, ra_sems)
-    mixed = cross[...]
-    lower.scatter(total[...] + (mixed + mixed.T))
+    mixed = total[:, 2 * rank:]
+    lower.scatter(total[:, 0:2 * rank] + (mixed + mixed.T))
     late = []
     for mask in (2, 3, 1) + tuple(range(4, n_src)):
         for q in range(per):
@@ -318,8 +316,7 @@
             pltpu.VMEM((tiles, rank + rank // 2, tile), f32),
             pltpu.VMEM((tiles, total_rank, tile), f32),
             pltpu.VMEM((3, tiles, rank // 2, tile), f32),
-            pltpu.VMEM((low, low), f32),
-            pltpu.VMEM((low, low), f32),
+            pltpu.VMEM((low, 2 * low), f32),
             pltpu.VMEM((n_tgt, low // n_tgt, low), f32),
             pltpu.VMEM((n_tgt - 1, low // n_tgt, low), f32),
             pltpu.VMEM((low // n_tgt, low), f32),
@@ -390,9 +387,13 @@
                 [rows(mask, 0), rows(mask - mask % 2, 1), rows(mask - mask % 4, 2)], axis=0)
             coarse[mask, :, 0, q * tile:(q + 1) * tile] = product(coarse_w[mask], operand)
         put_coarse(mask).start()
+    w_high, w_low = split(middle_w[...])
+    wide = jnp.concatenate([jnp.concatenate([w_high, w_high], axis=1),
+                            jnp.concatenate([w_low, jnp.zeros_like(w_low)], axis=1)], axis=0)
     for j in range(tiles):
         fetch(j).wait()
-        middle[j] = product(middle_w[...], stack[j])
+        value = jnp.dot(wide, jnp.concatenate(split(stack[j]), axis=0), preferred_element_type=jnp.float32)
+        middle[j] = value[0:rank] + value[rank:]
         put_middle(j).start()
     for mask in range(n_src):
         put_coarse(mask).wait()

time: 53.7 us -> 53.7 us (level)
  no operation moved by 1% of the time
where the time goes in v4:
time: 53.7 us; the launch traced here: 53.5 us
  Pallas kernels  52.8 us (98%)
  between operations  0.64 us (1%)
    pallas_call x1, Pallas kernels, gather(): pl.pallas_call(functools.partial(gather_kernel, n_src, n_tgt, tiles, tile...  45.8 us
    pallas_call x1, Pallas kernels, finish(): pl.pallas_call(functools.partial(finish_kernel, n_src, tiles, tile, rank)...  7.04 us

profile of v4, /device:TPU:1, one launch (start us, length us, event | category | flops | bytes accessed | tf_op | source)
XLA Modules:
  0.0 53.5 jit_solution(9793968288282750237)
XLA Ops:
  0.6 45.8 %gather.1 = (f32[8,192,512]{2,1,0:T(8,128)}, f32[3,2,192,512]{3,2,1,0:T(8,128)}, f32[64,128]{1,0:T(8,128)}, f32[4,64,192]{2,1,0:T(8,128)}) custom-call(bf16[4096,2048]{1,0:T(8,128)(2,1)} %kernel_hbm.1, bf16[192,2048]{1,0:T(8,128)(2,1)} %bitcast.1), custom_call_target="tpu_custom_call" | custom-call | tf_op jit(solution)/shard_map/gather/pallas_call | solution.py:304
  46.4 7.0 %finish.1 = (f32[1,64,4096]{2,1,0:T(8,128)}, f32[4,64,1,1024]{3,2,1,0:T(1,128)}) custom-call(f32[8,192,512]{2,1,0:T(8,128)} %get-tuple-element.6.stack_hbm, f32[3,2,192,512]{3,2,1,0:T(8,128)} %get-tuple-element.7.moved_hbm, f32[64,128]{1,0:T(8,128)} %get-tuple-element.8.middle_w, f32[4,64,192]{2,1,0:T(8,128)} %get-tuple-element.9.coarse_w), custom_call_target="tpu_custom_call" | custom-call | tf_op jit(solution)/shard_map/finish/pallas_call | solution.py:413
